TPU v7x, 128 devices: a whole 4x4x4 slice. The times are simulated.
128 devices in a mesh: expert: 16 (over y, x), edata: 8 (over z, core).
Axes of the slice: x: 4, y: 4, z: 4, core: 2. Of those that a mesh axis runs over, the one named last changes fastest.
Arguments:
- out_grad: bfloat16 [131072, 4096], P(('expert', 'edata')), may hold values from -3.5 to 3.5
- hidden_saved: bfloat16 [131072, 768], P(('expert', 'edata')), may hold values from -6 to 6
- recv_counts: int32 [2048], P(('expert', 'edata')), may hold values from 1 to 64, as said below
- master_weight: float32 [65536, 768], P(('expert', 'edata'))
- moment_one: bfloat16 [65536, 768], P(('expert', 'edata')), may hold values from -4 to 4
- moment_two: bfloat16 [65536, 768], P(('expert', 'edata')), may hold values from 0.049804688 to 0.5
Outputs:
- new_master: float32 [65536, 768], P(('expert', 'edata'))
- new_moment_one: bfloat16 [65536, 768], P(('expert', 'edata'))
- new_moment_two: bfloat16 [65536, 768], P(('expert', 'edata'))
- scaled_weight: bfloat16 [65536, 768], P('expert')
- expert_peak: float32 [16], P('expert')
Inputs may be any that keep to these rules, and one draw needn't show every extreme that they name: `recv_counts`: counts are skewed over experts; in every draw some pair fills all 64 slots.
All inputs are finite; a program needn't handle non-finite values. Where the computation divides by a largest or mean magnitude, that divisor is 1e-20 or more.
Results may differ from a plain program's by a relative error of at most 0.001.
Values may be sent and summed in bfloat16 or wider, within the bound.
A program may use at most 128 MiB of HBM per device.

v0:
```python
import jax
import jax.numpy as jnp
from jax import lax
from jax.sharding import PartitionSpec as P

beta_one = 0.9
beta_two = 0.999
correct_one = 1.0 - 0.9**5
correct_two = 1.0 - 0.999**5
adam_eps = 1e-08
learn_rate = 0.05
weight_decay = 1.0
peak_eps = 1e-06


def local(out_grad, hidden_saved, recv_counts, master_weight, moment_one, moment_two):
    experts = lax.axis_size("expert")
    capacity = out_grad.shape[0] // experts
    arrived = lax.all_to_all(out_grad, "expert", split_axis=0, concat_axis=0, tiled=True)
    slots = jnp.arange(capacity)
    live = (slots[None, :] < recv_counts[:, None]).reshape(-1)
    masked = jnp.where(live[:, None], arrived, jnp.zeros((), jnp.bfloat16))
    grad = lax.psum_scatter(
        lax.dot_general(
            masked, hidden_saved, (((0,), (0,)), ((), ())), preferred_element_type=jnp.float32
        ),
        "edata",
        scatter_dimension=0,
        tiled=True,
    )
    first = beta_one * moment_one.astype(jnp.float32) + (1.0 - beta_one) * grad
    second = beta_two * moment_two.astype(jnp.float32) + (1.0 - beta_two) * grad * grad
    update = first / correct_one / (jnp.sqrt(second / correct_two) + adam_eps)
    new_master = master_weight - learn_rate * (update + weight_decay * master_weight)
    local_peak = jnp.max(jnp.abs(new_master))
    peak = lax.pmax(local_peak, "edata")
    scaled_shard = (new_master / (peak + peak_eps)).astype(jnp.bfloat16)
    scaled = lax.all_gather(scaled_shard, "edata", axis=0, tiled=True)
    return (
        new_master,
        first.astype(jnp.bfloat16),
        second.astype(jnp.bfloat16),
        scaled,
        peak.reshape(1),
    )


def solution(mesh):
    placed = (
        P(("expert", "edata"), None),
        P(("expert", "edata"), None),
        P(("expert", "edata")),
        P(("expert", "edata"), None),
        P(("expert", "edata"), None),
        P(("expert", "edata"), None),
    )
    return jax.shard_map(
        local,
        mesh=mesh,
        in_specs=placed,
        out_specs=(
            P(("expert", "edata"), None),
            P(("expert", "edata"), None),
            P(("expert", "edata"), None),
            P("expert", None),
            P("expert"),
        ),
        check_vma=False,
    )
```

profile of v0, /device:TPU:1, one launch (start us, length us, event | category | flops | bytes accessed | tf_op | source)
XLA Modules:
  0.0 306.5 jit_solution(4694745972800328352)
XLA Ops:
  7.2 0.0 copy-start
  7.2 0.0 copy-start.2
  7.2 7.8 %all-to-all-start = ((bf16[16,64,4096]{2,1,0:T(8,128)(2,1)}), bf16[16,64,4096]{2,1,0:T(8,128)(2,1)}, u32[]{:S(2)}, u32[]{:S(2)}) async-start(bf16[16,64,4096]{2,1,0:T(8,128)(2,1)} %bitcast.6), calls=%async_computation | async-start | bytes 16777216 | tf_op jit(solution)/shard_map/all_to_all | solution.py:19
  15.0 0.0 reduce-scatter.2.cloned.1.call-start
  15.0 0.0 copy-done.2
  15.0 0.1 iota_compare_fusion
  15.1 0.1 lt.23
  15.2 123.1 %all-to-all-done = bf16[16,64,4096]{2,1,0:T(8,128)(2,1)} async-done(((bf16[16,64,4096]{2,1,0:T(8,128)(2,1)}), bf16[16,64,4096]{2,1,0:T(8,128)(2,1)}, u32[]{:S(2)}, u32[]{:S(2)}) %all-to-all-start) | async-done | bytes 8388640 | tf_op jit(solution)/shard_map/all_to_all | solution.py:19
  138.3 7.2 %bitcast_select_fusion = bf16[1024,4096]{1,0:T(8,128)(2,1)} fusion(bf16[16,64,4096]{2,1,0:T(8,128)(2,1)} %all-to-all-done, pred[1024]{0:T(1024)(128)(4,1)S(1)} %lt.23), kind=kLoop, calls=%fused_computation | loop fusion | flops 4194304 | bytes 16778240 | tf_op jit(solution)/shard_map/jit(_where)/select_n | solution.py:22
  145.5 0.0 copy-done
  145.5 12.9 %fusion.3 = f32[4096,768]{1,0:T(8,128)} fusion(bf16[1024,4096]{1,0:T(8,128)(2,1)} %bitcast_select_fusion, bf16[1024,768]{1,0:T(8,128)(2,1)S(1)} %copy-done), kind=kOutput, calls=%fused_computation.10 | convolution fusion | flops 6442450944 | bytes 22544384 | tf_op jit(solution)/shard_map/dot_general | solution.py:24
  158.4 0.0 reduce-scatter.2.cloned.1.call-update
  158.4 0.0 all-gather.2.cloned.1.call-start
  158.5 74.1 %reduce-scatter.2.cloned.1.call-done = f32[512,768]{1,0:T(8,128)} async-done(((f32[4096,768]{1,0:T(8,128)}), f32[512,768]{1,0:T(8,128)}) %reduce-scatter.2.cloned.1.call-update) | async-done | bytes 1572880 | tf_op jit(solution)/shard_map/reduce_scatter | solution.py:23
  232.5 5.4 %abs_reduce_fusion = (f32[]{:T(128)}, f32[512,768]{1,0:T(8,128)S(1)}, bf16[512,768]{1,0:T(8,128)(2,1)}, bf16[512,768]{1,0:T(8,128)(2,1)}) fusion(f32[512,768]{1,0:T(8,128)} %param.9, f32[512,768]{1,0:T(8,128)} %reduce-scatter.2.cloned.1.call-done, bf16[512,768]{1,0:T(8,128)(2,1)} %param.11, bf16[512,768]{1,0:T(8,128)(2,1)} %param.10), kind=kLoop, calls=%fused_computation.4 | loop fusion | flops 7864319 | bytes 7864324 | tf_op jit(solution)/shard_map/reduce_max | solution.py:35
  238.0 0.0 copy-start.1
  238.0 13.8 %pmax.7 = f32[]{:T(128)} all-reduce(f32[]{:T(128)} %get-tuple-element.5), channel_id=1, replica_groups=mesh['expert'=16,'edata'=8] {'edata'}, use_global_device_ids=true, to_apply=%region_2.3 | all-reduce | flops 1 | bytes 8 | tf_op jit(solution)/shard_map/pmax | solution.py:36
  252.4 1.0 divide_convert_fusion
  253.4 0.0 all-gather.2.cloned.1.call-update
  253.4 0.0 copy-done.1
  253.4 40.4 %all-gather.2.cloned.1.call-done = bf16[4096,768]{1,0:T(8,128)(2,1)} async-done(((bf16[512,768]{1,0:T(8,128)(2,1)}), bf16[4096,768]{1,0:T(8,128)(2,1)}) %all-gather.2.cloned.1.call-update) | async-done | bytes 6291472 | tf_op jit(solution)/shard_map/all_gather | solution.py:38
  293.8 5.9 %copy.12 = bf16[4096,768]{1,0:T(8,128)(2,1)} copy(bf16[4096,768]{1,0:T(8,128)(2,1)} %all-gather.2.cloned.1.call-done) | data formatting | bytes 12582912
Async XLA Ops:
  7.2 138.4 %copy-start = (bf16[1024,768]{1,0:T(8,128)(2,1)S(1)}, bf16[1024,768]{1,0:T(8,128)(2,1)}, u32[]{:S(2)}) copy-start(bf16[1024,768]{1,0:T(8,128)(2,1)} %param.7) | copy-start | bytes 4718596
  7.2 7.8 %copy-start.2 = (s32[16]{0:T(128)S(1)}, s32[16]{0:T(128)}, u32[]{:S(2)}) copy-start(s32[16]{0:T(128)} %param.8) | copy-start | bytes 196
  7.2 131.1 %all-to-all-start = ((bf16[16,64,4096]{2,1,0:T(8,128)(2,1)}), bf16[16,64,4096]{2,1,0:T(8,128)(2,1)}, u32[]{:S(2)}, u32[]{:S(2)}) async-start(bf16[16,64,4096]{2,1,0:T(8,128)(2,1)} %bitcast.6), calls=%async_computation | async-start | bytes 16777216 | tf_op jit(solution)/shard_map/all_to_all | solution.py:19
  15.0 217.6 %reduce-scatter.2.cloned.1.call-start = ((), (), s32[]{:S(2)}) async-start(), calls=%async_computation.2 | async-start | bytes 14155776 | tf_op jit(solution)/shard_map/reduce_scatter | solution.py:23
  158.4 135.4 %all-gather.2.cloned.1.call-start = ((), (), s32[]{:S(2)}) async-start(), calls=%async_computation.3 | async-start | bytes 7077888 | tf_op jit(solution)/shard_map/all_gather | solution.py:38
  238.0 15.4 %copy-start.1 = (f32[512,768]{1,0:T(8,128)}, f32[512,768]{1,0:T(8,128)S(1)}, u32[]{:S(2)}) copy-start(f32[512,768]{1,0:T(8,128)S(1)} %get-tuple-element.14) | copy-start | bytes 4718596
Sparse Core Ops, SparseCore 0:
  158.5 73.9 reduce-scatter.1
  253.5 40.2 all-gather.1
where the time goes:
time: 307 us
  waiting for transfers between devices  238 us (78%)
  between operations  14.7 us (5%)
  blocking collectives  13.8 us (4%)
  other arithmetic  13.7 us (4%)
  matrix products  12.9 us (4%)
  starting transfers between devices  7.85 us (3%)
  local copies, waits for them, and re-layouts  6 us (2%)
    all_to_all x1, waiting for transfers between devices, local(): lax.all_to_all(out_grad, 'expert', split_axis=0, concat_axis=0, tiled=True)  123 us
    reduce_scatter x1, waiting for transfers between devices, local(): lax.psum_scatter(lax.dot_general(masked, hidden_saved, (((0,), (0,)), (()...  74.1 us
    all_gather x1, waiting for transfers between devices, local(): scaled = lax.all_gather(scaled_shard, 'edata', axis=0, tiled=True)  40.4 us
    pmax x1, blocking collectives, local(): peak = lax.pmax(local_peak, 'edata')  13.8 us
    dot_general x1, matrix products, local(): lax.dot_general(masked, hidden_saved, (((0,), (0,)), ((), ())), preferred...  12.9 us
    all_to_all x1, starting transfers between devices, local(): lax.all_to_all(out_grad, 'expert', split_axis=0, concat_axis=0, tiled=True)  7.77 us
    select_n x1, other arithmetic, local(): masked = jnp.where(live[:, None], arrived, jnp.zeros((), jnp.bfloat16))  7.22 us
  transfers between devices with their start and end apart: 3, of which 3 were waited for; matrix products, arithmetic and copies ran while one was open for 0% of the time, Pallas kernels for 0%

commit v1 on v0

--- a/solution.py
+++ b/solution.py
@@ -35,7 +35,10 @@
     local_peak = jnp.max(jnp.abs(new_master))
     peak = lax.pmax(local_peak, "edata")
     scaled_shard = (new_master / (peak + peak_eps)).astype(jnp.bfloat16)
-    scaled = lax.all_gather(scaled_shard, "edata", axis=0, tiled=True)
+    n_dev = lax.axis_size("edata")
+    blocks = jnp.stack([scaled_shard for _ in range(n_dev)])
+    blocks = lax.all_to_all(blocks, "edata", split_axis=0, concat_axis=0)
+    scaled = jnp.concatenate(blocks, axis=0)
     return (
         new_master,
         first.astype(jnp.bfloat16),

time: 307 us -> 337 us (1.098)
  blocking collectives: 13.8 us -> 88.1 us
  waiting for transfers between devices: 238 us -> 197 us
    all_to_all x0 -> x1, blocking collectives: none -> 74.3 us  [local(): blocks = lax.all_to_all(blocks, 'edata', split_axis=0, concat_axis=0)]
    all_gather x1 -> x0, waiting for transfers between devices: 40.4 us -> none  [local(): scaled = lax.all_gather(scaled_shard, 'edata', axis=0, tiled=True)]
  transfers between devices with their start and end apart: 3 -> 2, of which waited for: 3 -> 2; matrix products, arithmetic and copies ran while one was open for 0% -> 0% of each run, Pallas kernels for 0% -> 0%
where the time goes in v1:
time: 337 us
  waiting for transfers between devices  197 us (58%)
  blocking collectives  88.1 us (26%)
  between operations  14.7 us (4%)
  matrix products  12.9 us (4%)
  other arithmetic  12.8 us (4%)
  starting transfers between devices  7.81 us (2%)
    all_to_all x1, waiting for transfers between devices, local(): lax.all_to_all(out_grad, 'expert', split_axis=0, concat_axis=0, tiled=True)  123 us
    all_to_all x1, blocking collectives, local(): blocks = lax.all_to_all(blocks, 'edata', split_axis=0, concat_axis=0)  74.3 us
    reduce_scatter x1, waiting for transfers between devices, local(): lax.psum_scatter(lax.dot_general(masked, hidden_saved, (((0,), (0,)), (()...  74.1 us
    pmax x1, blocking collectives, local(): peak = lax.pmax(local_peak, 'edata')  13.8 us
    dot_general x1, matrix products, local(): lax.dot_general(masked, hidden_saved, (((0,), (0,)), ((), ())), preferred...  12.9 us
    all_to_all x1, starting transfers between devices, local(): lax.all_to_all(out_grad, 'expert', split_axis=0, concat_axis=0, tiled=True)  7.77 us
    select_n x1, other arithmetic, local(): masked = jnp.where(live[:, None], arrived, jnp.zeros((), jnp.bfloat16))  7.21 us
  transfers between devices with their start and end apart: 2, of which 2 were waited for; matrix products, arithmetic and copies ran while one was open for 0% of the time, Pallas kernels for 0%

profile of v1, /device:TPU:1, one launch (start us, length us, event | category | flops | bytes accessed | tf_op | source)
XLA Modules:
  0.0 336.8 jit_solution(9706345110864537874)
XLA Ops:
  7.2 0.0 copy-start
  7.2 0.0 copy-start.2
  7.2 7.8 %all-to-all-start = ((bf16[16,64,4096]{2,1,0:T(8,128)(2,1)}), bf16[16,64,4096]{2,1,0:T(8,128)(2,1)}, u32[]{:S(2)}, u32[]{:S(2)}) async-start(bf16[16,64,4096]{2,1,0:T(8,128)(2,1)} %bitcast.8), calls=%async_computation | async-start | bytes 16777216 | tf_op jit(solution)/shard_map/all_to_all | solution.py:19
  15.0 0.0 reduce-scatter.2.cloned.1.call-start
  15.0 0.0 copy-done.2
  15.0 0.1 iota_compare_fusion
  15.1 0.1 lt.23
  15.2 123.1 %all-to-all-done = bf16[16,64,4096]{2,1,0:T(8,128)(2,1)} async-done(((bf16[16,64,4096]{2,1,0:T(8,128)(2,1)}), bf16[16,64,4096]{2,1,0:T(8,128)(2,1)}, u32[]{:S(2)}, u32[]{:S(2)}) %all-to-all-start) | async-done | bytes 8388640 | tf_op jit(solution)/shard_map/all_to_all | solution.py:19
  138.3 7.2 %bitcast_select_fusion = bf16[1024,4096]{1,0:T(8,128)(2,1)} fusion(bf16[16,64,4096]{2,1,0:T(8,128)(2,1)} %all-to-all-done, pred[1024]{0:T(1024)(128)(4,1)S(1)} %lt.23), kind=kLoop, calls=%fused_computation | loop fusion | flops 4194304 | bytes 16778240 | tf_op jit(solution)/shard_map/jit(_where)/select_n | solution.py:22
  145.5 0.0 copy-done
  145.5 12.9 %fusion.3 = f32[4096,768]{1,0:T(8,128)} fusion(bf16[1024,4096]{1,0:T(8,128)(2,1)} %bitcast_select_fusion, bf16[1024,768]{1,0:T(8,128)(2,1)S(1)} %copy-done), kind=kOutput, calls=%fused_computation.10 | convolution fusion | flops 6442450944 | bytes 22544384 | tf_op jit(solution)/shard_map/dot_general | solution.py:24
  158.4 0.0 reduce-scatter.2.cloned.1.call-update
  158.4 74.1 %reduce-scatter.2.cloned.1.call-done = f32[512,768]{1,0:T(8,128)} async-done(((f32[4096,768]{1,0:T(8,128)}), f32[512,768]{1,0:T(8,128)}) %reduce-scatter.2.cloned.1.call-update) | async-done | bytes 1572880 | tf_op jit(solution)/shard_map/reduce_scatter | solution.py:23
  232.5 5.4 %abs_reduce_fusion = (f32[]{:T(128)}, f32[512,768]{1,0:T(8,128)S(1)}, bf16[512,768]{1,0:T(8,128)(2,1)}, bf16[512,768]{1,0:T(8,128)(2,1)}) fusion(f32[512,768]{1,0:T(8,128)} %param.9, f32[512,768]{1,0:T(8,128)} %reduce-scatter.2.cloned.1.call-done, bf16[512,768]{1,0:T(8,128)(2,1)} %param.11, bf16[512,768]{1,0:T(8,128)(2,1)} %param.10), kind=kLoop, calls=%fused_computation.4 | loop fusion | flops 7864319 | bytes 7864324 | tf_op jit(solution)/shard_map/reduce_max | solution.py:35
  238.0 0.0 copy-start.1
  238.0 13.8 %pmax.7 = f32[]{:T(128)} all-reduce(f32[]{:T(128)} %get-tuple-element.5), channel_id=1, replica_groups=mesh['expert'=16,'edata'=8] {'edata'}, use_global_device_ids=true, to_apply=%region_2.3 | all-reduce | flops 1 | bytes 8 | tf_op jit(solution)/shard_map/pmax | solution.py:36
  252.4 0.1 divide_convert_fusion
  252.5 0.4 stack.2
  252.9 0.0 copy-done.1
  252.9 74.3 %all_to_all.17 = bf16[8,512,768]{2,1,0:T(8,128)(2,1)S(1)} all-to-all(bf16[8,512,768]{2,1,0:T(8,128)(2,1)S(1)} %stack.2), channel_id=1, replica_groups=mesh['expert'=16,'edata'=8] {'edata'}, dimensions={0} | all-to-all | bytes 12582912 | tf_op jit(solution)/shard_map/all_to_all | solution.py:40
  327.2 2.7 copy.12
Async XLA Ops:
  7.2 138.4 %copy-start = (bf16[1024,768]{1,0:T(8,128)(2,1)S(1)}, bf16[1024,768]{1,0:T(8,128)(2,1)}, u32[]{:S(2)}) copy-start(bf16[1024,768]{1,0:T(8,128)(2,1)} %param.7) | copy-start | bytes 4718596
  7.2 7.8 %copy-start.2 = (s32[16]{0:T(128)S(1)}, s32[16]{0:T(128)}, u32[]{:S(2)}) copy-start(s32[16]{0:T(128)} %param.8) | copy-start | bytes 196
  7.2 131.1 %all-to-all-start = ((bf16[16,64,4096]{2,1,0:T(8,128)(2,1)}), bf16[16,64,4096]{2,1,0:T(8,128)(2,1)}, u32[]{:S(2)}, u32[]{:S(2)}) async-start(bf16[16,64,4096]{2,1,0:T(8,128)(2,1)} %bitcast.8), calls=%async_computation | async-start | bytes 16777216 | tf_op jit(solution)/shard_map/all_to_all | solution.py:19
  15.0 217.6 %reduce-scatter.2.cloned.1.call-start = ((), (), s32[]{:S(2)}) async-start(), calls=%async_computation.3 | async-start | bytes 14155776 | tf_op jit(solution)/shard_map/reduce_scatter | solution.py:23
  238.0 15.0 %copy-start.1 = (f32[512,768]{1,0:T(8,128)}, f32[512,768]{1,0:T(8,128)S(1)}, u32[]{:S(2)}) copy-start(f32[512,768]{1,0:T(8,128)S(1)} %get-tuple-element.14) | copy-start | bytes 4718596
Sparse Core Ops, SparseCore 0:
  158.5 73.9 reduce-scatter.1
